TPU v7x, 512 devices: a whole 4x4x16 slice. The times are simulated.
512 devices in a mesh: ctx: 32 (over y_lo, z), fsdp: 16 (over x, y_hi, core).
Axes of the slice: x: 4, y: 4 (y_hi: 2, y_lo: 2; y = y_hi * 2 + y_lo), z: 16, core: 2. Of those that a mesh axis runs over, the one named last changes fastest.
Arguments:
- hidden_in: bfloat16 [16, 8192, 4096], P('fsdp', 'ctx'), may hold values from -40 to 40
- page_tokens: int32 [16, 16], P('fsdp'), may hold values from 1 to 1280, 8192 in all within a row
- grad_attn: bfloat16 [16, 8192, 128], P('fsdp', 'ctx'), may hold values from -6 to 6
- w_qkv: bfloat16 [4096, 384], P('fsdp'), may hold values from -1 to 1
Outputs:
- grad_hidden: bfloat16 [16, 8192, 4096], P('fsdp', 'ctx')
- grad_w_qkv: float32 [4096, 384], P('fsdp')
Inputs may be any that keep to these rules, and one draw needn't show every extreme that they name: `page_tokens`: each document's page lengths sum to 8192.
All inputs are finite; a program needn't handle non-finite values.
Results may differ from a plain program's by a relative error of at most 0.039.
Values may be sent and summed in bfloat16 or wider, within the bound.
A program may use at most 128 MiB of HBM per device.

v0:
```python
import jax
import jax.numpy as jnp
from jax import lax
from jax.sharding import PartitionSpec as P


def page_limits(page_row, positions, total_len):
    page_ends = jnp.cumsum(page_row)
    return jnp.min(
        jnp.where(page_ends[None, :] > positions[:, None], page_ends[None, :], total_len), axis=1
    )


def dot_rows(left, right):
    return lax.dot_general(
        left, right, (((1,), (1,)), ((), ())), preferred_element_type=jnp.float32
    )


def dot_cols(left, right):
    return lax.dot_general(
        left, right, (((0,), (0,)), ((), ())), preferred_element_type=jnp.float32
    )


def local(hidden_in, page_tokens, grad_attn, w_qkv):
    inputs_dev = hidden_in[0]
    grad_out = grad_attn[0]
    page_row = page_tokens[0]
    tok_rows = inputs_dev.shape[0]
    head_width = grad_out.shape[1]
    seq_len = tok_rows * lax.axis_size("ctx")
    score_scale = head_width ** (-0.5)
    weights_all = lax.all_gather(w_qkv, "fsdp", axis=0, tiled=True)
    projected = jnp.dot(inputs_dev, weights_all, preferred_element_type=jnp.float32)
    projected = projected.astype(jnp.bfloat16)
    queries = projected[:, :head_width]
    keys_own = projected[:, head_width : 2 * head_width]
    values_own = projected[:, 2 * head_width :]
    keys_all, values_all = (
        lax.all_gather(keys_own, "ctx", axis=0, tiled=True),
        lax.all_gather(values_own, "ctx", axis=0, tiled=True),
    )
    first_pos = lax.axis_index("ctx") * tok_rows
    positions = first_pos + jnp.arange(tok_rows, dtype=jnp.int32)
    limits = page_limits(page_row, positions, seq_len)
    key_pos = jnp.arange(seq_len, dtype=jnp.int32)
    visible = key_pos[None, :] < limits[:, None]
    scores = jnp.where(visible, dot_rows(queries, keys_all) * score_scale, -1e30)
    row_max = jnp.max(scores, axis=1, keepdims=True)
    log_total = row_max[:, 0] + jnp.log(jnp.sum(jnp.exp(scores - row_max), axis=1))
    probs_full = jnp.exp(scores - log_total[:, None])
    probs_half = probs_full.astype(jnp.bfloat16)
    attended = jnp.dot(probs_half, values_all, preferred_element_type=jnp.float32)
    out_dot = jnp.sum(grad_out.astype(jnp.float32) * attended, axis=1)
    dprob = dot_rows(grad_out, values_all)
    dscore = (probs_full * (dprob - out_dot[:, None]) * score_scale).astype(jnp.bfloat16)
    query_grad = jnp.dot(dscore, keys_all, preferred_element_type=jnp.float32)
    q_piece = lax.all_gather(queries.astype(jnp.float32), "ctx", axis=0, tiled=True).astype(
        jnp.bfloat16
    )
    grad_piece = lax.all_gather(grad_out.astype(jnp.float32), "ctx", axis=0, tiled=True).astype(
        jnp.bfloat16
    )
    total_piece = lax.all_gather(log_total, "ctx", axis=0, tiled=True)
    dot_piece = lax.all_gather(out_dot, "ctx", axis=0, tiled=True)
    piece_rows = q_piece.shape[0]
    piece_limits = page_limits(page_row, jnp.arange(piece_rows, dtype=jnp.int32), seq_len)
    seen = positions[None, :] < piece_limits[:, None]
    piece_scores = jnp.where(seen, dot_rows(q_piece, keys_own) * score_scale, -1e30)
    piece_probs = jnp.exp(piece_scores - total_piece[:, None])
    piece_half = piece_probs.astype(jnp.bfloat16)
    piece_dprob = dot_rows(grad_piece, values_own)
    piece_dscore = (piece_probs * (piece_dprob - dot_piece[:, None]) * score_scale).astype(
        jnp.bfloat16
    )
    key_grad = dot_cols(piece_dscore, q_piece)
    value_grad = dot_cols(piece_half, grad_piece)
    grad_qkv = jnp.concatenate([query_grad, key_grad, value_grad], axis=1).astype(jnp.bfloat16)
    grad_inputs = dot_rows(grad_qkv, weights_all)
    grad_inputs = grad_inputs.astype(jnp.bfloat16)[None]
    block_term = dot_cols(inputs_dev, grad_qkv).astype(jnp.bfloat16)
    block_sum = lax.psum_scatter(
        lax.optimization_barrier(block_term).astype(jnp.float32).astype(jnp.bfloat16),
        "fsdp",
        scatter_dimension=0,
        tiled=True,
    ).astype(jnp.float32)
    grad_weights = lax.psum(block_sum, "ctx")
    return (grad_inputs, grad_weights)


def solution(mesh):
    in_specs = (P("fsdp", "ctx", None), P("fsdp", None), P("fsdp", "ctx", None), P("fsdp", None))
    out_specs = (P("fsdp", "ctx", None), P("fsdp", None))
    return jax.shard_map(local, mesh=mesh, in_specs=in_specs, out_specs=out_specs, check_vma=False)
```

profile of v0, /device:TPU:8, one launch (start us, length us, event | category | flops | bytes accessed | tf_op | source)
XLA Modules:
  0.0 845.2 jit_solution(10110642753795459561)
XLA Ops:
  7.2 0.0 copy-start
  7.2 0.0 copy-start.3
  7.2 0.0 copy-start.4
  7.2 0.0 all-gather.8.cloned.1.call-start
  7.2 0.7 all-gather.8.cloned.1.call-update
  7.9 0.0 all-gather.10.cloned.1.call-start
  8.0 74.5 %all-gather.8.cloned.1.call-done = bf16[4096,384]{1,0:T(8,128)(2,1)} async-done(((bf16[256,384]{1,0:T(8,128)(2,1)}), bf16[4096,384]{1,0:T(8,128)(2,1)}) %all-gather.8.cloned.1.call-update) | async-done | bytes 3145744 | tf_op jit(solution)/shard_map/all_gather | solution.py:34
  82.5 0.0 copy-done
  82.5 3.1 fusion.25
  85.7 0.7 fusion.54
  86.3 0.0 all-gather.10.cloned.1.call-update
  86.4 0.0 all-gather.12.cloned.1.call-start
  86.4 0.7 all-gather.12.cloned.1.call-update
  87.1 0.0 all-gather.14.cloned.1.call-start
  87.1 0.5 all-gather.14.cloned.1.call-update
  87.7 0.0 all-gather.16.cloned.1.call-start
  87.7 0.0 copy-done.3
  87.7 0.7 copy.18
  88.5 0.0 all-gather.16.cloned.1.call-update
  88.5 0.0 reduce-scatter.2.cloned.1.call-start
  88.5 0.0 copy-done.4
  88.5 0.1 copy.17
  88.7 0.1 reduce
  88.8 0.1 select_reduce_fusion.1
  88.9 0.2 select_reduce_fusion
  89.1 129.8 %all-gather.10.cloned.1.call-done = bf16[8192,128]{1,0:T(8,128)(2,1)} async-done(((bf16[256,128]{1,0:T(8,128)(2,1)}), bf16[8192,128]{1,0:T(8,128)(2,1)}) %all-gather.10.cloned.1.call-update) | async-done | bytes 2097168 | tf_op jit(solution)/shard_map/all_gather | solution.py:41
  218.9 3.3 fusion.55
  222.2 0.0 copy-start.1
  222.2 0.0 copy-start.2
  222.2 1.3 exponential_reduce_fusion
  223.6 1.8 copy-done.1
  225.5 123.1 %all-gather.12.cloned.1.call-done = bf16[8192,128]{1,0:T(8,128)(2,1)} async-done(((bf16[256,128]{1,0:T(8,128)(2,1)}), bf16[8192,128]{1,0:T(8,128)(2,1)}) %all-gather.12.cloned.1.call-update) | async-done | bytes 2097168 | tf_op jit(solution)/shard_map/all_gather | solution.py:42
  348.6 0.0 copy-done.2
  348.6 5.7 fusion.36
  354.3 61.5 %all-gather.1 = f32[32,1,256]{2,1,0:T(1,128)S(1)} all-gather(f32[1,1,256]{2,1,0:T(1,128)S(1)} %bitcast.63), channel_id=1, replica_groups=mesh['ctx'=32,'fsdp'=16] {'ctx'}, dimensions={0}, use_global_device_ids=true | all-gather | bytes 33792 | tf_op jit(solution)/shard_map/all_gather | solution.py:66
  415.8 58.6 %all-gather = f32[32,1,256]{2,1,0:T(1,128)S(1)} all-gather(f32[1,1,256]{2,1,0:T(1,128)S(1)} %bitcast.62), channel_id=1, replica_groups=mesh['ctx'=32,'fsdp'=16] {'ctx'}, dimensions={0}, use_global_device_ids=true | all-gather | bytes 33792 | tf_op jit(solution)/shard_map/all_gather | solution.py:65
  474.4 3.6 all-gather.14.cloned.1.call-done
  478.1 7.7 fusion.9
  485.7 7.2 fusion.31
  492.9 109.0 %all-gather.16.cloned.1.call-done = bf16[8192,128]{0,1:T(8,128)(2,1)} async-done(((bf16[256,128]{0,1:T(8,128)(2,1)}), bf16[8192,128]{0,1:T(8,128)(2,1)}) %all-gather.16.cloned.1.call-update) | async-done | bytes 2097168 | tf_op jit(solution)/shard_map/all_gather | solution.py:62
  601.9 4.7 fusion.32
  606.6 7.1 fusion.35
  613.7 2.7 fusion.13
  616.3 0.0 reduce-scatter.2.cloned.1.call-update
  616.4 4.5 fusion.14
  620.9 89.6 %reduce-scatter.2.cloned.1.call-done = bf16[256,384]{0,1:T(8,128)(2,1)} async-done(((bf16[4096,384]{0,1:T(8,128)(2,1)}), bf16[256,384]{0,1:T(8,128)(2,1)}) %reduce-scatter.2.cloned.1.call-update) | async-done | bytes 196624 | tf_op jit(solution)/shard_map/reduce_scatter | solution.py:83
  710.5 126.9 %all-reduce.1 = f32[256,384]{0,1:T(8,128)S(1)} all-reduce(bf16[256,384]{0,1:T(8,128)(2,1)} %reduce-scatter.2.cloned.1.call-done), channel_id=1, replica_groups=mesh['ctx'=32,'fsdp'=16] {'ctx'}, use_global_device_ids=true, to_apply=%region_7.8 | all-reduce | flops 98304 | bytes 589824 | tf_op jit(solution)/shard_map/psum | solution.py:89
  837.4 0.9 copy.21
  (3 shorter events, 0.0 us)
Async XLA Ops:
  7.2 75.3 %copy-start = (bf16[1,256,4096]{2,1,0:T(8,128)(2,1)S(1)}, bf16[1,256,4096]{2,1,0:T(8,128)(2,1)}, u32[]{:S(2)}) copy-start(bf16[1,256,4096]{2,1,0:T(8,128)(2,1)} %param.4) | copy-start | bytes 6291460
  7.2 80.5 %copy-start.3 = (bf16[1,256,128]{2,1,0:T(8,128)(2,1)S(1)}, bf16[1,256,128]{2,1,0:T(8,128)(2,1)}, u32[]{:S(2)}) copy-start(bf16[1,256,128]{2,1,0:T(8,128)(2,1)} %param.6) | copy-start | bytes 196612
  7.2 81.3 %copy-start.4 = (s32[1,16]{1,0:T(1,128)S(1)}, s32[1,16]{1,0:T(1,128)}, u32[]{:S(2)}) copy-start(s32[1,16]{1,0:T(1,128)} %param.5) | copy-start | bytes 196
  7.2 75.3 %all-gather.8.cloned.1.call-start = ((), (), s32[]{:S(2)}) async-start(), calls=%async_computation.1 | async-start | bytes 3342336 | tf_op jit(solution)/shard_map/all_gather | solution.py:34
  7.9 211.0 %all-gather.10.cloned.1.call-start = ((), (), s32[]{:S(2)}) async-start(), calls=%async_computation.2 | async-start | bytes 2162688 | tf_op jit(solution)/shard_map/all_gather | solution.py:41
  86.4 262.2 %all-gather.12.cloned.1.call-start = ((), (), s32[]{:S(2)}) async-start(), calls=%async_computation.3 | async-start | bytes 2162688 | tf_op jit(solution)/shard_map/all_gather | solution.py:42
  87.1 391.0 %all-gather.14.cloned.1.call-start = ((), (), s32[]{:S(2)}) async-start(), calls=%async_computation.4 | async-start | bytes 2162688 | tf_op jit(solution)/shard_map/all_gather | solution.py:59
  87.7 514.2 %all-gather.16.cloned.1.call-start = ((), (), s32[]{:S(2)}) async-start(), calls=%async_computation.5 | async-start | bytes 2162688 | tf_op jit(solution)/shard_map/all_gather | solution.py:62
  88.5 622.0 %reduce-scatter.2.cloned.1.call-start = ((), (), s32[]{:S(2)}) async-start(), calls=%async_computation.6 | async-start | bytes 3342336 | tf_op jit(solution)/shard_map/reduce_scatter | solution.py:83
  222.2 3.2 copy-start.1
  222.2 126.3 %copy-start.2 = (bf16[1,256,128]{1,2,0:T(8,128)(2,1)S(1)}, bf16[1,256,128]{1,2,0:T(8,128)(2,1)}, u32[]{:S(2)}) copy-start(bf16[1,256,128]{1,2,0:T(8,128)(2,1)} %copy.18) | copy-start | bytes 196612
Sparse Core Ops, SparseCore 0:
  11.3 71.1 all-gather.7
  86.5 132.4 all-gather.9
  221.6 126.9 all-gather.11
  351.1 126.9 all-gather.13
  479.9 121.9 all-gather.15
  616.5 93.9 reduce-scatter.1
where the time goes:
time: 846 us; the launch traced here: 845 us
  waiting for transfers between devices  532 us (63%)
  blocking collectives  247 us (29%)
  matrix products  45.9 us (5%)
  between operations  14.2 us (2%)
    all_gather x1, waiting for transfers between devices, local(): lax.all_gather(keys_own, 'ctx', axis=0, tiled=True)  130 us
    psum x1, blocking collectives, local(): grad_weights = lax.psum(block_sum, 'ctx')  127 us
    all_gather x1, waiting for transfers between devices, local(): lax.all_gather(values_own, 'ctx', axis=0, tiled=True)  123 us
    all_gather x1, waiting for transfers between devices, local(): lax.all_gather(grad_out.astype(jnp.float32), 'ctx', axis=0, tiled=True)  109 us
    reduce_scatter x1, waiting for transfers between devices, local(): lax.psum_scatter(lax.optimization_barrier(block_term).astype(jnp.float32)...  89.6 us
    all_gather x1, waiting for transfers between devices, local(): weights_all = lax.all_gather(w_qkv, 'fsdp', axis=0, tiled=True)  74.5 us
    all_gather x1, blocking collectives, local(): dot_piece = lax.all_gather(out_dot, 'ctx', axis=0, tiled=True)  61.5 us
    all_gather x1, blocking collectives, local(): total_piece = lax.all_gather(log_total, 'ctx', axis=0, tiled=True)  58.6 us
  transfers between devices with their start and end apart: 6, of which 6 were waited for; matrix products, arithmetic and copies ran while one was open for 4% of the time, Pallas kernels for 0%

commit v1 on v0

--- a/solution.py
+++ b/solution.py
@@ -31,7 +31,9 @@
     head_width = grad_out.shape[1]
     seq_len = tok_rows * lax.axis_size("ctx")
     score_scale = head_width ** (-0.5)
-    weights_all = lax.all_gather(w_qkv, "fsdp", axis=0, tiled=True)
+    weights_all = jnp.concatenate(
+        lax.all_to_all(jnp.stack([w_qkv] * lax.axis_size("fsdp")), "fsdp", 0, 0), axis=0
+    )
     projected = jnp.dot(inputs_dev, weights_all, preferred_element_type=jnp.float32)
     projected = projected.astype(jnp.bfloat16)
     queries = projected[:, :head_width]

time: 846 us -> 819 us (0.968)
  waiting for transfers between devices: 532 us -> 458 us
  blocking collectives: 247 us -> 293 us
    all_gather x1 -> x0, waiting for transfers between devices: 74.5 us -> none  [local(): weights_all = lax.all_gather(w_qkv, 'fsdp', axis=0, tiled=True)]
    all_to_all x0 -> x1, blocking collectives: none -> 46.4 us  [local(): lax.all_to_all(jnp.stack([w_qkv] * lax.axis_size('fsdp')), 'fsdp', 0, 0)]
  transfers between devices with their start and end apart: 6 -> 5, of which waited for: 6 -> 5; matrix products, arithmetic and copies ran while one was open for 4% -> 4% of each run, Pallas kernels for 0% -> 0%
where the time goes in v1:
time: 819 us; the launch traced here: 818 us
  waiting for transfers between devices  458 us (56%)
  blocking collectives  293 us (36%)
  matrix products  44.1 us (5%)
  between operations  13.9 us (2%)
    all_gather x1, waiting for transfers between devices, local(): lax.all_gather(keys_own, 'ctx', axis=0, tiled=True)  131 us
    psum x1, blocking collectives, local(): grad_weights = lax.psum(block_sum, 'ctx')  127 us
    all_gather x1, waiting for transfers between devices, local(): lax.all_gather(values_own, 'ctx', axis=0, tiled=True)  123 us
    all_gather x1, waiting for transfers between devices, local(): lax.all_gather(grad_out.astype(jnp.float32), 'ctx', axis=0, tiled=True)  109 us
    reduce_scatter x1, waiting for transfers between devices, local(): lax.psum_scatter(lax.optimization_barrier(block_term).astype(jnp.float32)...  89.8 us
    all_gather x1, blocking collectives, local(): dot_piece = lax.all_gather(out_dot, 'ctx', axis=0, tiled=True)  61.5 us
    all_gather x1, blocking collectives, local(): total_piece = lax.all_gather(log_total, 'ctx', axis=0, tiled=True)  58.6 us
    all_to_all x1, blocking collectives, local(): lax.all_to_all(jnp.stack([w_qkv] * lax.axis_size('fsdp')), 'fsdp', 0, 0)  46.4 us
  transfers between devices with their start and end apart: 5, of which 5 were waited for; matrix products, arithmetic and copies ran while one was open for 4% of the time, Pallas kernels for 0%

profile of v1, /device:TPU:8, one launch (start us, length us, event | category | flops | bytes accessed | tf_op | source)
XLA Modules:
  0.0 818.5 jit_solution(14436294717102385232)
XLA Ops:
  7.2 0.0 copy-start
  7.2 0.0 all-gather.7.cloned.1.call-start
  7.2 1.5 stack.2
  8.7 46.4 %all_to_all.5 = bf16[16,256,384]{2,1,0:T(8,128)(2,1)S(1)} all-to-all(bf16[16,256,384]{2,1,0:T(8,128)(2,1)S(1)} %stack.2), channel_id=1, replica_groups=mesh['ctx'=32,'fsdp'=16] {'fsdp'}, dimensions={0} | all-to-all | bytes 6291456 | tf_op jit(solution)/shard_map/all_to_all | solution.py:35
  55.1 0.0 copy-start.2
  55.1 0.0 copy-start.4
  55.1 0.0 copy-start.5
  55.1 1.7 copy-done.2
  56.8 0.0 copy-done
  56.8 1.3 fusion.25
  58.1 0.7 fusion.54
  58.7 0.0 all-gather.7.cloned.1.call-update
  58.8 0.0 all-gather.9.cloned.1.call-start
  58.8 0.7 all-gather.9.cloned.1.call-update
  59.5 0.0 all-gather.11.cloned.1.call-start
  59.6 0.7 all-gather.11.cloned.1.call-update
  60.2 0.0 all-gather.13.cloned.1.call-start
  60.3 0.0 copy-done.4
  60.3 0.7 copy.18
  61.0 0.0 all-gather.13.cloned.1.call-update
  61.1 0.0 reduce-scatter.2.cloned.1.call-start
  61.1 0.0 copy-done.5
  61.1 0.1 copy.17
  61.2 0.1 reduce
  61.4 0.1 select_reduce_fusion.1
  61.5 0.2 select_reduce_fusion
  61.7 130.7 %all-gather.7.cloned.1.call-done = bf16[8192,128]{1,0:T(8,128)(2,1)} async-done(((bf16[256,128]{1,0:T(8,128)(2,1)}), bf16[8192,128]{1,0:T(8,128)(2,1)}) %all-gather.7.cloned.1.call-update) | async-done | bytes 2097168 | tf_op jit(solution)/shard_map/all_gather | solution.py:43
  192.4 3.3 fusion.55
  195.7 0.0 copy-start.1
  195.7 0.0 copy-start.3
  195.7 1.3 exponential_reduce_fusion
  197.0 1.8 copy-done.1
  198.9 123.1 %all-gather.9.cloned.1.call-done = bf16[8192,128]{1,0:T(8,128)(2,1)} async-done(((bf16[256,128]{1,0:T(8,128)(2,1)}), bf16[8192,128]{1,0:T(8,128)(2,1)}) %all-gather.9.cloned.1.call-update) | async-done | bytes 2097168 | tf_op jit(solution)/shard_map/all_gather | solution.py:44
  322.0 0.0 copy-done.3
  322.0 5.7 fusion.36
  327.7 61.5 %all-gather.1 = f32[32,1,256]{2,1,0:T(1,128)S(1)} all-gather(f32[1,1,256]{2,1,0:T(1,128)S(1)} %bitcast.66), channel_id=1, replica_groups=mesh['ctx'=32,'fsdp'=16] {'ctx'}, dimensions={0}, use_global_device_ids=true | all-gather | bytes 33792 | tf_op jit(solution)/shard_map/all_gather | solution.py:68
  389.2 58.6 %all-gather = f32[32,1,256]{2,1,0:T(1,128)S(1)} all-gather(f32[1,1,256]{2,1,0:T(1,128)S(1)} %bitcast.65), channel_id=1, replica_groups=mesh['ctx'=32,'fsdp'=16] {'ctx'}, dimensions={0}, use_global_device_ids=true | all-gather | bytes 33792 | tf_op jit(solution)/shard_map/all_gather | solution.py:67
  447.8 3.8 all-gather.11.cloned.1.call-done
  451.6 7.7 fusion.9
  459.3 7.2 fusion.31
  466.4 108.9 %all-gather.13.cloned.1.call-done = bf16[8192,128]{0,1:T(8,128)(2,1)} async-done(((bf16[256,128]{0,1:T(8,128)(2,1)}), bf16[8192,128]{0,1:T(8,128)(2,1)}) %all-gather.13.cloned.1.call-update) | async-done | bytes 2097168 | tf_op jit(solution)/shard_map/all_gather | solution.py:64
  575.3 4.7 fusion.32
  580.0 7.1 fusion.35
  587.1 2.7 fusion.13
  589.8 0.0 reduce-scatter.2.cloned.1.call-update
  589.8 4.5 fusion.14
  594.3 89.8 %reduce-scatter.2.cloned.1.call-done = bf16[256,384]{0,1:T(8,128)(2,1)} async-done(((bf16[4096,384]{0,1:T(8,128)(2,1)}), bf16[256,384]{0,1:T(8,128)(2,1)}) %reduce-scatter.2.cloned.1.call-update) | async-done | bytes 196624 | tf_op jit(solution)/shard_map/reduce_scatter | solution.py:85
  684.1 126.9 %all-reduce.1 = f32[256,384]{0,1:T(8,128)S(1)} all-reduce(bf16[256,384]{0,1:T(8,128)(2,1)} %reduce-scatter.2.cloned.1.call-done), channel_id=1, replica_groups=mesh['ctx'=32,'fsdp'=16] {'ctx'}, use_global_device_ids=true, to_apply=%region_7.8 | all-reduce | flops 98304 | bytes 589824 | tf_op jit(solution)/shard_map/psum | solution.py:91
  811.0 0.9 copy.21
  (3 shorter events, 0.0 us)
Async XLA Ops:
  7.2 49.6 %copy-start = (bf16[1,256,4096]{2,1,0:T(8,128)(2,1)S(1)}, bf16[1,256,4096]{2,1,0:T(8,128)(2,1)}, u32[]{:S(2)}) copy-start(bf16[1,256,4096]{2,1,0:T(8,128)(2,1)} %param.4) | copy-start | bytes 6291460
  7.2 185.2 %all-gather.7.cloned.1.call-start = ((), (), s32[]{:S(2)}) async-start(), calls=%async_computation.2 | async-start | bytes 2162688 | tf_op jit(solution)/shard_map/all_gather | solution.py:43
  55.1 1.7 copy-start.2
  55.1 5.2 copy-start.4
  55.1 6.0 copy-start.5
  58.8 263.2 %all-gather.9.cloned.1.call-start = ((), (), s32[]{:S(2)}) async-start(), calls=%async_computation.3 | async-start | bytes 2162688 | tf_op jit(solution)/shard_map/all_gather | solution.py:44
  59.5 392.1 %all-gather.11.cloned.1.call-start = ((), (), s32[]{:S(2)}) async-start(), calls=%async_computation.4 | async-start | bytes 2162688 | tf_op jit(solution)/shard_map/all_gather | solution.py:61
  60.2 515.1 %all-gather.13.cloned.1.call-start = ((), (), s32[]{:S(2)}) async-start(), calls=%async_computation.5 | async-start | bytes 2162688 | tf_op jit(solution)/shard_map/all_gather | solution.py:64
  61.1 623.0 %reduce-scatter.2.cloned.1.call-start = ((), (), s32[]{:S(2)}) async-start(), calls=%async_computation.6 | async-start | bytes 3342336 | tf_op jit(solution)/shard_map/reduce_scatter | solution.py:85
  195.7 3.2 copy-start.1
  195.7 126.3 %copy-start.3 = (bf16[1,256,128]{1,2,0:T(8,128)(2,1)S(1)}, bf16[1,256,128]{1,2,0:T(8,128)(2,1)}, u32[]{:S(2)}) copy-start(bf16[1,256,128]{1,2,0:T(8,128)(2,1)} %copy.18) | copy-start | bytes 196612
Sparse Core Ops, SparseCore 0:
  58.9 133.4 all-gather.6
  195.0 126.9 all-gather.8
  324.7 126.9 all-gather.10
  453.5 121.7 all-gather.12
  589.9 94.1 reduce-scatter.1
